TPU v7x, 32 devices: a whole 2x2x4 slice. The times are simulated.
32 devices in a mesh: box: 32 (over z, y, x, core).
Axes of the slice: x: 2, y: 2, z: 4, core: 2. Of those that a mesh axis runs over, the one named last changes fastest.
Arguments:
- basis_vector: float32 [16, 131072], P(None, 'box'), may hold values from -600 to 600
- diagonal: float32 [131072], P('box'), may hold values from 0.25 to 2
- coords: int32 [2, 131072], P(None, 'box'), may hold values from 0 to 4095
- phase_scale: int32 [1], replicated, may hold values from 1 to 8190
- sketch_rows: int32 [131072], P('box'), may hold values from 0 to 2047
- sketch_signs: int32 [131072], P('box'), may hold values from 0 to 1
Outputs:
- new_basis: float32 [16, 131072], P(None, 'box')
- sketch: float32 [16, 2048], replicated
- arnoldi: float32 [2, 16], replicated
All inputs are finite; a program needn't handle non-finite values.
Results may differ from a plain program's by a relative error of at most 0.00019.
Values sent between devices are 32-bit elements; how exact they have to be, the bound alone decides.
A program may use at most 64 MiB of HBM per device.

v0:
```python
import math

import jax
import jax.numpy as jnp
from jax import lax
from jax.sharding import PartitionSpec as P

RANK = 16
WIDTH = 32
LEAF = 32
SKETCH = 2048


modulus = 8191
epsilon = 1e-06


def swapped(x, axis, bit):
    return lax.ppermute(x, axis, [(i, i ^ 1 << bit) for i in range(lax.axis_size(axis))])


def leaf_table(coords, phase_scale):
    scale_mod = phase_scale[0] % modulus
    freq = jnp.arange(RANK, dtype=jnp.int32)
    freq_first = freq % 4 + 1
    freq_second = freq // 4 + 1
    linear = (
        freq_first[:, None] * coords[0][None, :] + freq_second[:, None] * coords[1][None, :]
    ) % modulus
    phase = scale_mod * linear % modulus
    angle = phase.astype(jnp.float32) * (2.0 * math.pi / modulus)
    return jnp.concatenate([jnp.cos(angle), jnp.sin(angle)], 0) * (1.0 / math.sqrt(LEAF))


def translations(box_ids, segment_num, phase_scale):
    scale_mod = phase_scale[0] % modulus
    base_key = (box_ids * 37 + 101 * segment_num) % (modulus - 1) + 1
    unit_phase = scale_mod * base_key % modulus
    indices = jnp.arange(WIDTH, dtype=jnp.int32)
    prod_a = (indices[:, None] + 1) * (indices[None, :] + 2) % modulus
    prod_b = (indices[:, None] + 3) * (indices[None, :] + 1) % modulus
    phase_a = prod_a[:, :, None] * unit_phase[None, None, :] % modulus
    phase_b = (prod_b[:, :, None] * unit_phase[None, None, :] + 4096) % modulus
    factor = 2.0 * math.pi / modulus
    ident = jnp.eye(WIDTH, dtype=jnp.float32)[:, :, None]
    own_map = 0.85 * ident + 0.35 / math.sqrt(WIDTH) * jnp.cos(phase_a.astype(jnp.float32) * factor)
    cross_map = 0.6 / math.sqrt(WIDTH) * jnp.cos(phase_b.astype(jnp.float32) * factor)
    return (own_map, cross_map)


def mix(matrix, coeffs):
    return jnp.einsum("wvg,vgq->wgq", matrix, coeffs, precision=lax.Precision.HIGHEST)


def one_segment(coeffs, segment_num, group_boxes, phase_scale):
    own_map, cross_map = translations(group_boxes, segment_num, phase_scale)
    partner = swapped(coeffs, "box", segment_num)
    return mix(own_map, coeffs) + mix(cross_map, partner)


def body(basis_vector, diagonal, coords, phase_scale, sketch_rows, sketch_signs):
    highest = lax.Precision.HIGHEST
    columns, local_points = basis_vector.shape
    box_count = local_points // LEAF
    devices = lax.axis_size("box")
    segment_count = devices.bit_length() - 1
    rank_id = lax.axis_index("box")
    local_ids = jnp.arange(box_count, dtype=jnp.int32)
    group_boxes = rank_id * box_count + local_ids
    leaf_map = leaf_table(coords, phase_scale)
    leaf_boxes = leaf_map.reshape(WIDTH, box_count, LEAF)
    blocks = basis_vector.reshape(columns, box_count, LEAF)
    coeffs = jnp.einsum("wgs,qgs->wgq", leaf_boxes, blocks, precision=highest)
    for segment_num in range(segment_count):
        coeffs = one_segment(coeffs, segment_num, group_boxes, phase_scale)
    applied = jnp.einsum("wgs,wgq->qgs", leaf_boxes, coeffs, precision=highest).reshape(
        columns, local_points
    )
    image = diagonal[None, :] * basis_vector + applied
    total_points = local_points * devices
    sketch_factor = math.sqrt(SKETCH / total_points)
    sign_values = (2 * sketch_signs - 1).astype(jnp.float32)
    block_rows = math.gcd(local_points, 512)
    block_count = local_points // block_rows
    row_blocks = sketch_rows.reshape(block_count, block_rows)
    sketch_ids = jnp.arange(SKETCH, dtype=jnp.int32)

    def sketch_of(values):
        signed = (values * sign_values[None, :]).reshape(columns, block_count, block_rows)
        signed = jnp.transpose(signed, (1, 0, 2))

        def add_block(total, pieces):
            piece, rows_here = pieces
            onehot = (rows_here[:, None] == sketch_ids[None, :]).astype(jnp.float32)
            return (
                total
                + jnp.dot(piece, onehot, precision=highest, preferred_element_type=jnp.float32),
                None,
            )

        total, unused = lax.scan(
            add_block, jnp.zeros((columns, SKETCH), jnp.float32), (signed, row_blocks)
        )
        return total

    sketch_image, sketch_basis, inner_sum, square_sum, energy_sum = lax.psum(
        (
            sketch_of(image),
            sketch_of(basis_vector),
            jnp.sum(basis_vector * image, axis=1),
            jnp.sum(basis_vector * basis_vector, axis=1),
            jnp.sum(image * image, axis=1),
        ),
        "box",
    )
    inner_vw = inner_sum / total_points
    raw_square = square_sum / total_points
    projection = inner_vw / (raw_square + epsilon)
    energy = (
        energy_sum / total_points
        - 2.0 * projection * inner_vw
        + projection * projection * raw_square
    )
    spread = jnp.sqrt(energy + epsilon)
    residual = image - projection[:, None] * basis_vector
    new_basis = residual / spread[:, None]
    sketch = (sketch_image - projection[:, None] * sketch_basis) * sketch_factor / spread[:, None]
    arnoldi = jnp.stack([projection, spread])
    return (new_basis, sketch, arnoldi)


def solution(mesh):
    placed = (P(None, "box"), P("box"), P(None, "box"), P(), P("box"), P("box"))
    return jax.shard_map(
        body, mesh=mesh, in_specs=placed, out_specs=(P(None, "box"), P(), P()), check_vma=False
    )
```

profile of v0, /device:TPU:0, one launch (start us, length us, event | category | flops | bytes accessed | tf_op | source)
XLA Modules:
  0.0 354.1 jit_solution(480010976030757982)
XLA Ops:
  10.5 1.8 copy.18
  13.7 5.1 %fusion.125 = f32[32,128,16]{0,2,1:T(8,128)S(1)} fusion(f32[32,128,32]{2,0,1:T(8,128)S(1)} %copy.18, f32[16,128,32]{2,1,0:T(8,128)} %reshape.278), kind=kOutput, calls=%fused_computation.127 | convolution fusion | flops 25296896 | bytes 1048576 | tf_op jit(solution)/shard_map/wgs,qgs->wgq/dot_general | solution.py:73
  27.7 14.8 %fusion.21 = f32[128,16,32]{2,1,0:T(8,128)} fusion(f32[32,128,16]{0,2,1:T(8,128)S(1)} %fusion.125, s32[128]{0:T(128)} %and_select_fusion.8, s32[32,32]{1,0:T(8,128)S(1)} %get-tuple-element.126, f32[32,32]{1,0:T(8,128)} %fusion.249), kind=kOutput, calls=%fused_computation.33 | convolution fusion | flops 26607616 | bytes 532992 | tf_op jit(solution)/shard_map/wvg,vgq->wgq/dot_general | solution.py:52
  42.6 2.4 copy.21
  45.0 13.4 %fusion.158 = f32[32,128,16]{0,2,1:T(8,128)S(1)} fusion(f32[128,16,32]{2,1,0:T(8,128)} %fusion.21, f32[32,128,16]{0,2,1:T(8,128)} %copy.21, s32[32,32]{1,0:T(8,128)} %get-tuple-element.125, s32[128]{0:T(128)} %and_select_fusion.8), kind=kOutput, calls=%fused_computation.138 | convolution fusion | flops 26673152 | bytes 791040 | tf_op jit(solution)/shard_map/wvg,vgq->wgq/dot_general | solution.py:52
  59.5 2.5 collective-permute-start.1
  62.0 14.7 %fusion.34 = f32[128,16,32]{2,1,0:T(8,128)} fusion(f32[32,128,16]{0,2,1:T(8,128)S(1)} %fusion.158, s32[128]{0:T(128)} %and_select_fusion.6, s32[32,32]{1,0:T(8,128)} %copy-done.7, f32[32,32]{1,0:T(8,128)} %fusion.249), kind=kOutput, calls=%fused_computation.44 | convolution fusion | flops 26607616 | bytes 532992 | tf_op jit(solution)/shard_map/wvg,vgq->wgq/dot_general | solution.py:52
  76.7 2.4 copy.23
  79.1 13.3 %fusion.152 = f32[32,128,16]{0,2,1:T(8,128)S(1)} fusion(f32[128,16,32]{2,1,0:T(8,128)} %fusion.34, f32[32,128,16]{0,2,1:T(8,128)} %copy.23, s32[128]{0:T(128)} %and_select_fusion.6, s32[32,32]{1,0:T(8,128)} %get-tuple-element.125), kind=kOutput, calls=%fused_computation.136 | convolution fusion | flops 26673152 | bytes 791040 | tf_op jit(solution)/shard_map/wvg,vgq->wgq/dot_general | solution.py:52
  95.1 14.9 %fusion.47 = f32[128,16,32]{2,1,0:T(8,128)} fusion(f32[32,128,16]{0,2,1:T(8,128)S(1)} %fusion.152, s32[128]{0:T(128)} %and_select_fusion.4, s32[32,32]{1,0:T(8,128)} %copy-done.7, f32[32,32]{1,0:T(8,128)} %fusion.249), kind=kOutput, calls=%fused_computation.55 | convolution fusion | flops 26607616 | bytes 532992 | tf_op jit(solution)/shard_map/wvg,vgq->wgq/dot_general | solution.py:52
  110.0 2.4 copy.25
  112.4 13.3 %fusion.146 = f32[32,128,16]{0,2,1:T(8,128)S(1)} fusion(f32[128,16,32]{2,1,0:T(8,128)} %fusion.47, f32[32,128,16]{0,2,1:T(8,128)} %copy.25, s32[128]{0:T(128)} %and_select_fusion.4, s32[32,32]{1,0:T(8,128)} %get-tuple-element.125), kind=kOutput, calls=%fused_computation.134 | convolution fusion | flops 26673152 | bytes 791040 | tf_op jit(solution)/shard_map/wvg,vgq->wgq/dot_general | solution.py:52
  128.5 14.7 %fusion.60 = f32[128,16,32]{2,1,0:T(8,128)} fusion(f32[32,128,16]{0,2,1:T(8,128)S(1)} %fusion.146, s32[128]{0:T(128)} %and_select_fusion.2, s32[32,32]{1,0:T(8,128)} %copy-done.7, f32[32,32]{1,0:T(8,128)} %fusion.249), kind=kOutput, calls=%fused_computation.66 | convolution fusion | flops 26607616 | bytes 532992 | tf_op jit(solution)/shard_map/wvg,vgq->wgq/dot_general | solution.py:52
  143.2 2.4 copy.27
  145.6 13.3 %fusion.140 = f32[32,128,16]{0,2,1:T(8,128)S(1)} fusion(f32[128,16,32]{2,1,0:T(8,128)} %fusion.60, f32[32,128,16]{0,2,1:T(8,128)} %copy.27, s32[128]{0:T(128)} %and_select_fusion.2, s32[32,32]{1,0:T(8,128)} %get-tuple-element.125), kind=kOutput, calls=%fused_computation.132 | convolution fusion | flops 26673152 | bytes 791040 | tf_op jit(solution)/shard_map/wvg,vgq->wgq/dot_general | solution.py:52
  160.1 2.6 collective-permute-start.4
  162.7 14.9 %fusion.73 = f32[128,16,32]{2,1,0:T(8,128)} fusion(f32[32,128,16]{0,2,1:T(8,128)S(1)} %fusion.140, s32[128]{0:T(128)} %and_select_fusion, s32[32,32]{1,0:T(8,128)} %copy-done.7, f32[32,32]{1,0:T(8,128)} %fusion.249), kind=kOutput, calls=%fused_computation.77 | convolution fusion | flops 26607616 | bytes 532992 | tf_op jit(solution)/shard_map/wvg,vgq->wgq/dot_general | solution.py:52
  179.1 14.2 %fusion.134 = f32[32,128,16]{0,2,1:T(8,128)S(1)} fusion(f32[128,16,32]{2,1,0:T(8,128)} %fusion.73, f32[32,128,16]{0,2,1:T(8,128)S(1)} %copy.29, s32[128]{0:T(128)} %and_select_fusion, s32[32,32]{1,0:T(8,128)} %get-tuple-element.125), kind=kOutput, calls=%fused_computation.130 | convolution fusion | flops 26673152 | bytes 791040 | tf_op jit(solution)/shard_map/wvg,vgq->wgq/dot_general | solution.py:52
  193.3 2.1 fusion.128
  196.5 12.0 %while.22 = (s32[]{:T(128)}, f32[16,2048]{1,0:T(8,128)S(1)}, f32[8,16,512]{2,1,0:T(8,128)S(1)}, s32[8,512]{1,0:T(8,128)S(1)}, s32[]{:T(128)}, /*index=5*/s32[]{:T(128)}) while((s32[]{:T(128)}, f32[16,2048]{1,0:T(8,128)S(1)}, f32[8,16,512]{2,1,0:T(8,128)S(1)}, s32[8,512]{1,0:T(8,128)S(1)}, s32[]{:T(128)}, /*index=5*/s32[]{:T(128)}) %tuple.64), condition=%wide.region_7.8_spmd.clone, body=%wide.region_6.7_spmd.clone.sunk | while | flops 202440704 | bytes 301151 | solution.py:101
  209.2 11.9 %while.23 = (s32[]{:T(128)}, f32[16,2048]{1,0:T(8,128)S(1)}, f32[8,16,512]{2,1,0:T(8,128)S(1)}, s32[8,512]{1,0:T(8,128)S(1)}, s32[]{:T(128)}, /*index=5*/s32[]{:T(128)}) while((s32[]{:T(128)}, f32[16,2048]{1,0:T(8,128)S(1)}, f32[8,16,512]{2,1,0:T(8,128)S(1)}, s32[8,512]{1,0:T(8,128)S(1)}, s32[]{:T(128)}, ...), condition=%wide.region_10.11_spmd.clone, body=%wide.region_9.10_spmd.clone.sunk | while | flops 202440704 | bytes 301151 | solution.py:101
  221.8 38.2 %all-reduce = (f32[16]{0:T(128)S(1)}, f32[16]{0:T(128)S(1)}, f32[16]{0:T(128)S(1)}) all-reduce(f32[16]{0:T(128)S(1)} %get-tuple-element.95, f32[16]{0:T(128)S(1)} %get-tuple-element.94, f32[16]{0:T(128)S(1)} %get-tuple-element.93), channel_id=1, replica_groups=mesh['box'=32] {'box'}, use_global_device_ids=true, to_apply=%region_3.4 | all-reduce | flops 48 | bytes 384 | tf_op jit(solution)/shard_map/psum | solution.py:106
  261.4 83.7 %all-reduce.4.cloned.1.call-done = (f32[16,2048]{1,0:T(8,128)}, f32[16,2048]{1,0:T(8,128)}) async-done(((f32[16,2048]{1,0:T(8,128)}, f32[16,2048]{1,0:T(8,128)}), (f32[16,2048]{1,0:T(8,128)}, f32[16,2048]{1,0:T(8,128)})) %all-reduce.4.cloned.1.call-update) | async-done | bytes 262160 | tf_op jit(solution)/shard_map/psum | solution.py:106
  345.1 1.7 multiply_divide_fusion
  (94 shorter events, 49.7 us)
Async XLA Ops:
  7.2 337.9 %all-reduce.4.cloned.1.call-start = ((), (), s32[]{:S(2)}) async-start(), calls=%async_computation | async-start | bytes 524288 | tf_op jit(solution)/shard_map/psum | solution.py:106
  9.1 3.3 copy-start
  13.7 11.4 %copy-start.6 = (s32[4096]{0:T(1024)S(1)}, s32[4096]{0:T(1024)}, u32[]{:S(2)}) copy-start(s32[4096]{0:T(1024)} %param.15) | copy-start | bytes 49156
  20.0 22.6 %collective-permute-start = (f32[32,128,16]{1,2,0:T(8,128)}, f32[32,128,16]{1,2,0:T(8,128)}, u32[]{:S(2)}, u32[]{:S(2)}) collective-permute-start(f32[32,128,16]{1,2,0:T(8,128)} %copy.20), channel_id=1, source_target_pairs={{0,1},{1,0},{2,3},{3,2},{4,5},{5,4},{6,7},{7,6},{8,9},{9,8},{10,11... | collective-permute-start | bytes 786440 | tf_op jit(solution)/shard_map/ppermute | solution.py:19
  27.7 14.8 %copy-start.7 = (s32[32,32]{1,0:T(8,128)}, s32[32,32]{1,0:T(8,128)S(1)}, u32[]{:S(2)}) copy-start(s32[32,32]{1,0:T(8,128)S(1)} %get-tuple-element.126) | copy-start | bytes 12292
  59.5 17.1 %collective-permute-start.1 = (f32[32,128,16]{1,2,0:T(8,128)}, f32[32,128,16]{1,2,0:T(8,128)}, u32[]{:S(2)}, u32[]{:S(2)}) collective-permute-start(f32[32,128,16]{1,2,0:T(8,128)} %copy.22), channel_id=1, source_target_pairs={{0,2},{1,3},{2,0},{3,1},{4,6},{5,7},{6,4},{7,5},{8,10},{9,11},{10,... | collective-permute-start | bytes 786440 | tf_op jit(solution)/shard_map/ppermute | solution.py:19
  93.6 16.4 %collective-permute-start.2 = (f32[32,128,16]{1,2,0:T(8,128)}, f32[32,128,16]{1,2,0:T(8,128)}, u32[]{:S(2)}, u32[]{:S(2)}) collective-permute-start(f32[32,128,16]{1,2,0:T(8,128)} %copy.24), channel_id=1, source_target_pairs={{0,4},{1,5},{2,6},{3,7},{4,0},{5,1},{6,2},{7,3},{8,12},{9,13},{10,... | collective-permute-start | bytes 786440 | tf_op jit(solution)/shard_map/ppermute | solution.py:19
  126.9 16.2 %collective-permute-start.3 = (f32[32,128,16]{1,2,0:T(8,128)}, f32[32,128,16]{1,2,0:T(8,128)}, u32[]{:S(2)}, u32[]{:S(2)}) collective-permute-start(f32[32,128,16]{1,2,0:T(8,128)} %copy.26), channel_id=1, source_target_pairs={{0,8},{1,9},{2,10},{3,11},{4,12},{5,13},{6,14},{7,15},{8,0},{9,1},... | collective-permute-start | bytes 786440 | tf_op jit(solution)/shard_map/ppermute | solution.py:19
  160.1 17.5 %collective-permute-start.4 = (f32[32,128,16]{1,2,0:T(8,128)}, f32[32,128,16]{1,2,0:T(8,128)}, u32[]{:S(2)}, u32[]{:S(2)}) collective-permute-start(f32[32,128,16]{1,2,0:T(8,128)} %copy.28), channel_id=1, source_target_pairs={{0,16},{1,17},{2,18},{3,19},{4,20},{5,21},{6,22},{7,23},{8,24},{9,... | collective-permute-start | bytes 786440 | tf_op jit(solution)/shard_map/ppermute | solution.py:19
  195.4 0.9 copy-start.4
  195.4 0.9 copy-start.5
  195.4 1.1 copy-start.2
  208.5 0.7 copy-start.3
  221.1 0.7 copy-start.1
Sparse Core Ops, SparseCore 0:
  221.9 123.1 all-reduce.3
where the time goes:
time: 361 us; the launch traced here: 354 us
  matrix products  172 us (48%)
  waiting for transfers between devices  83.7 us (23%)
  blocking collectives  38.2 us (11%)
  local copies, waits for them, and re-layouts  24.3 us (7%)
  between operations  15.3 us (4%)
  other arithmetic  11.3 us (3%)
  starting transfers between devices  8.69 us (2%)
    dot_general x10, matrix products, mix(): jnp.einsum('wvg,vgq->wgq', matrix, coeffs, precision=lax.Precision.HIGHEST)  141 us
    psum x1, waiting for transfers between devices, body(): lax.psum((sketch_of(image), sketch_of(basis_vector), jnp.sum(basis_vector...  83.7 us
    psum x1, blocking collectives, body(): lax.psum((sketch_of(image), sketch_of(basis_vector), jnp.sum(basis_vector...  38.2 us
    dot_general x16, matrix products, add_block(): jnp.dot(piece, onehot, precision=highest, preferred_element_type=jnp.floa...  23.6 us
    ppermute x5, local copies, waits for them, and re-layouts, swapped(): lax.ppermute(x, axis, [(i, i ^ 1 << bit) for i in range(lax.axis_size(axi...  11.1 us
    ppermute x5, starting transfers between devices, swapped(): lax.ppermute(x, axis, [(i, i ^ 1 << bit) for i in range(lax.axis_size(axi...  8.65 us
  transfers between devices with their start and end apart: 6, of which 1 were waited for; matrix products, arithmetic and copies ran while one was open for 23% of the time, Pallas kernels for 0%

commit v1 on v0

v1 whole, which is shorter than its diff:
```python
import functools
import math

import jax
import jax.numpy as jnp
import numpy as np
from jax import lax
from jax.experimental import pallas as pl
from jax.experimental.pallas import tpu as pltpu
from jax.sharding import PartitionSpec as P

WIDTH = 32
LEAF = 32
SKETCH = 2048
LANES = 128
HIGH = 8
LOW = SKETCH // HIGH
MODULUS = 8191
EPSILON = 1e-06
MESH = pl.DeviceIdType.MESH
F32 = jnp.float32
BF16 = jnp.bfloat16


def sine_series():
    node = np.cos((np.arange(400) + 0.5) * np.pi / 800)
    basis = np.stack([node ** (2 * i) for i in range(6)], 1)
    exact = np.sin(np.pi * node * 4096 / MODULUS) / node
    return np.linalg.lstsq(basis, exact, rcond=None)[0]


SERIES = sine_series()


def remainder(n):
    return n - jnp.floor(n * (1.0 / MODULUS) + 0.5) * float(MODULUS)


def half_sine(n, gain):
    t = remainder(n) * (1.0 / 4096)
    z = t * t
    total = z * float(SERIES[5] * gain) + float(SERIES[4] * gain)
    for c in SERIES[3::-1]:
        total = total * z + float(c * gain)
    return total * t


def scaled_cos(n, amplitude):
    s = half_sine(n, math.sqrt(2.0 * amplitude))
    return amplitude - s * s


def scaled_sin(n, amplitude):
    return scaled_cos(n - 0.25 * MODULUS, amplitude)


def fold(p):
    return (p & MODULUS) + lax.shift_right_logical(p, 13)


def kernel(devices, stages, total_points, scale_ref, x_ref, nb_ref, sketch_ref, arn_ref,
           pts, leaf, mats, kk, cbuf, part, tbuf, work, onehot, skb, ski,
           a_send, a_recv, b_send, b_recv, sum_send, sum_recv, rs_send, rs_recv, ag_recv, own_chunk,
           a_ss, a_rs, b_ss, b_rs, s_ss, s_rs, r_ss, r_rs, g_ss, g_rs):
    me = lax.axis_index("box")
    columns = nb_ref.shape[0]
    halves = columns // 8
    barrier = pltpu.get_barrier_semaphore()

    @pl.loop(1, devices)
    def _(i):
        pl.semaphore_signal(barrier, inc=1, device_id=(lax.rem(me + i, devices),), device_id_type=MESH)

    lane = lax.broadcasted_iota(jnp.int32, (8, LANES), 1)
    sub = lax.broadcasted_iota(jnp.int32, (8, LANES), 0)
    scale = lax.rem(scale_ref[0], MODULUS)

    rows_in = x_ref.shape[0]
    for i in range(rows_in // 4):
        flipped = x_ref[4 * i:4 * i + 4].reshape(LANES, LANES).T
        tbuf[0] = flipped
        for j in range(4):
            pts[4 * i + j] = jnp.concatenate(
                [tbuf[0, 32 * g:32 * g + 32, 32 * j:32 * j + 32] for g in range(4)], axis=1)

    def exact_phase(row):
        return fold(pts[columns + row].astype(jnp.int32) * scale).astype(F32)

    work[0] = exact_phase(0)
    work[1] = exact_phase(1)
    fx = (sub % 4 + 1).astype(F32)
    fy = (sub // 4 + 1).astype(F32)
    unit = 1.0 / math.sqrt(LEAF)

    @pl.loop(0, LEAF)
    def _(s):
        px = work[0, pl.ds(s, 1), :]
        py = work[1, pl.ds(s, 1), :]
        for tile in range(2):
            n = fx * px + (fy + 2.0 * tile) * py
            leaf[s, 8 * tile:8 * tile + 8] = scaled_cos(n, unit)
            leaf[s, 16 + 8 * tile:24 + 8 * tile] = scaled_sin(n, unit)

    for h in range(halves):
        def gather(s, acc):
            tiles = [leaf[s, 8 * t:8 * t + 8] for t in range(4)]
            out = []
            for q in range(8):
                row = pts[8 * h + q, pl.ds(s, 1), :]
                for t in range(4):
                    out.append(acc[4 * q + t] + tiles[t] * row)
            return tuple(out)

        acc = lax.fori_loop(0, LEAF, gather, tuple(jnp.zeros((8, LANES), F32) for _ in range(32)), unroll=2)
        for q in range(8):
            for t in range(4):
                cbuf[pl.ds((8 * h + q) * 32 + 8 * t, 8), :] = acc[4 * q + t]

    blocks = columns * WIDTH // LANES

    def make_maps(low, bits):
        group = 2 ** bits
        places = LANES // group
        mine = lax.rem(me // 2 ** low, group)
        spot = mine * places + lane % places
        box = 4 * (spot % 32) + spot // 32
        member = me + (lane // places - mine) * 2 ** low
        ident = (member * LANES + box) * 37

        @pl.loop(low, low + bits)
        def _(k):
            x = (ident + 101 * k).astype(F32)
            rest = x - jnp.floor(x * (1.0 / (MODULUS - 1))) * float(MODULUS - 1)
            rest = jnp.where(rest < 0.0, rest + float(MODULUS - 1), rest)
            rest = jnp.where(rest >= float(MODULUS - 1), rest - float(MODULUS - 1), rest)
            key = rest.astype(jnp.int32) + 1
            unit_phase = fold(fold(key * scale)).astype(F32)
            wide = sub.astype(F32)
            for m in range(2):
                amplitude = (0.35 if m == 0 else 0.6) / math.sqrt(WIDTH)
                first, second, offset = (1.0, 2.0, 0.0) if m == 0 else (3.0, 1.0, 4096.0)
                mid = unit_phase * (wide + (8.0 + first))
                far = unit_phase * (wide + (16.0 + first))

                @pl.loop(0, WIDTH, unroll=2)
                def _(v):
                    times = v.astype(F32) + second
                    step = scaled_cos(unit_phase * (8.0 * times), 2.0)
                    one = scaled_cos(mid * times + offset, amplitude)
                    two = scaled_cos(far * times + offset, amplitude)
                    mats[2 * k + m, v, 8:16] = one
                    mats[2 * k + m, v, 16:24] = two
                    mats[2 * k + m, v, 0:8] = step * one - two
                    mats[2 * k + m, v, 24:32] = step * two - one

    def exchange(send, recv, ss, rs, low, bits, action):
        group = 2 ** bits
        mine = lax.rem(me // 2 ** low, group)

        @pl.loop(1, group)
        def _(i):
            other = lax.rem(mine + i, group)
            here = other if action is finish_recv else mine
            copy = pltpu.make_async_remote_copy(
                send.at[other], recv.at[here], ss.at[other], rs.at[here],
                device_id=(me + (other - mine) * 2 ** low,), device_id_type=MESH)
            action(copy)
        return mine

    def pack(send, group):
        places = LANES // group
        for j in range(blocks):
            tbuf[j] = cbuf[LANES * j:LANES * (j + 1), :].T
        for d in range(group):
            for j in range(blocks):
                send[d, places * j:places * (j + 1), :] = tbuf[j, places * d:places * (d + 1), :]

    def unpack(recv, group):
        places = LANES // group
        for j in range(blocks):
            for d in range(group):
                tbuf[j, places * d:places * (d + 1), :] = recv[d, places * j:places * (j + 1), :]
        for j in range(blocks):
            cbuf[LANES * j:LANES * (j + 1), :] = tbuf[j].T

    def sketch_of(values, target, make):
        target[...] = jnp.zeros_like(target)

        @pl.loop(0, LEAF // 4)
        def _(c):
            pieces = []
            for i in range(4):
                s = 4 * c + i
                row = pts[columns + 3, pl.ds(s, 1), :]
                high = jnp.floor(row * (1.0 / LOW))
                if make:
                    low = (row - high * LOW).astype(jnp.int32)
                    ids = lax.broadcasted_iota(jnp.int32, (LOW, LANES), 0)
                    onehot[c, :, LANES * i:LANES * (i + 1)] = jnp.where(ids == low, 1.0, 0.0).astype(BF16)
                sign = 2.0 * pts[columns + 4, pl.ds(s, 1), :] - 1.0
                v = values(s) * sign
                top = v.astype(BF16)
                rest = (v - top.astype(F32)).astype(BF16)
                wide = jnp.broadcast_to(high, (columns, LANES))
                masks = [jnp.where(wide == float(g), 1.0, 0.0).astype(BF16) for g in range(HIGH)]
                pieces.append(jnp.concatenate([top * g for g in masks] + [rest * g for g in masks], axis=0))
            left = jnp.concatenate(pieces, axis=1)
            target[...] += lax.dot_general(left, onehot[c], (((1,), (1,)), ((), ())), preferred_element_type=F32)

    nbt = kk

    def start(copy):
        copy.start()

    def finish_recv(copy):
        copy.wait_recv()

    def finish_send(copy):
        copy.wait_send()

    pl.semaphore_wait(barrier, devices - 1)
    for index, (low, bits) in enumerate(stages):
        group = 2 ** bits
        places = LANES // group
        send, recv, ssem, rsem = a_send.at[index], a_recv.at[index], a_ss.at[index], a_rs.at[index]
        pack(send, group)
        mine = exchange(send, recv, ssem, rsem, low, bits, start)
        recv[mine] = send[mine]
        make_maps(low, bits)
        if index == 0:
            for q in range(columns):
                for s in range(LEAF):
                    nbt[s, q:q + 1, :] = pts[q, s:s + 1, :]
            sketch_of(lambda s: nbt[s], skb, True)
        exchange(send, recv, ssem, rsem, low, bits, finish_recv)
        unpack(recv, group)
        for k in range(low, low + bits):
            span = places * 2 ** (k - low)
            full = cbuf[...]
            wide = lax.broadcasted_iota(jnp.int32, full.shape, 1)
            part[...] = jnp.where((wide // span) % 2 == 0,
                                  pltpu.roll(full, LANES - span, 1), pltpu.roll(full, span, 1))
            for h in range(halves):
                def mix(v, acc):
                    own = [mats[2 * k, v, 8 * t:8 * t + 8] for t in range(4)]
                    cross = [mats[2 * k + 1, v, 8 * t:8 * t + 8] for t in range(4)]
                    out = []
                    for q in range(8):
                        row = cbuf[pl.ds((8 * h + q) * 32 + v, 1), :]
                        other = part[pl.ds((8 * h + q) * 32 + v, 1), :]
                        for t in range(4):
                            out.append(acc[4 * q + t] + own[t] * row + cross[t] * other)
                    return tuple(out)

                init = tuple(0.85 * cbuf[pl.ds((8 * h + q) * 32 + 8 * t, 8), :] for q in range(8) for t in range(4))
                acc = lax.fori_loop(0, WIDTH, mix, init, unroll=2)
                for q in range(8):
                    for t in range(4):
                        cbuf[pl.ds((8 * h + q) * 32 + 8 * t, 8), :] = acc[4 * q + t]
        exchange(send, recv, ssem, rsem, low, bits, finish_send)
        send, recv, ssem, rsem = b_send.at[index], b_recv.at[index], b_ss.at[index], b_rs.at[index]
        pack(send, group)
        mine = exchange(send, recv, ssem, rsem, low, bits, start)
        recv[mine] = send[mine]
        exchange(send, recv, ssem, rsem, low, bits, finish_recv)
        unpack(recv, group)
        exchange(send, recv, ssem, rsem, low, bits, finish_send)

    for c in range(LEAF // 8):
        def spread_out(w, acc):
            coef = [cbuf[pl.ds(8 * h * 32 + w, 8, stride=32), :] for h in range(halves)]
            out = []
            for s in range(8):
                row = leaf[8 * c + s, pl.ds(w, 1), :]
                for h in range(halves):
                    out.append(acc[halves * s + h] + coef[h] * row)
            return tuple(out)

        init = tuple(
            jnp.broadcast_to(pts[columns + 2, 8 * c + s:8 * c + s + 1, :], (8, LANES)) * nbt[8 * c + s, 8 * h:8 * h + 8]
            for s in range(8) for h in range(halves))
        acc = lax.fori_loop(0, WIDTH, spread_out, init, unroll=2)
        for s in range(8):
            for h in range(halves):
                part[(8 * c + s) * columns + 8 * h:(8 * c + s) * columns + 8 * h + 8, :] = acc[halves * s + h]

    inner = jnp.zeros((columns, LANES), F32)
    square, energy = inner, inner
    for s in range(LEAF):
        v, image = nbt[s], part[s * columns:(s + 1) * columns, :]
        inner, square, energy = inner + v * image, square + v * v, energy + image * image
    lane_q = lax.broadcasted_iota(jnp.int32, (columns, LANES), 1)
    row_q = lax.broadcasted_iota(jnp.int32, (columns, LANES), 0)
    packed = jnp.zeros((columns, LANES), F32)
    for i, value in enumerate((inner, square, energy)):
        packed = jnp.where(lane_q == row_q + columns * i, jnp.sum(value, axis=1, keepdims=True), packed)
    sum_send[...] = jnp.sum(packed, axis=0, keepdims=True)

    def to_all(source, recv, ss, rs, action):
        @pl.loop(1, devices)
        def _(i):
            other = lax.rem(me + i, devices)
            here = other if action is finish_recv else me
            action(pltpu.make_async_remote_copy(
                source(other), recv.at[here], ss.at[other], rs.at[here],
                device_id=(other,), device_id_type=MESH))

    to_all(lambda d: sum_send, sum_recv, s_ss, s_rs, start)
    sum_recv[me] = sum_send[...]
    sketch_of(lambda s: part[pl.ds(pl.multiple_of(s * columns, columns), columns), :], ski, False)
    to_all(lambda d: sum_send, sum_recv, s_ss, s_rs, finish_recv)
    totals = jnp.sum(sum_recv[...], axis=0)

    def column(i):
        picked = jnp.where(lane_q == row_q + columns * i, jnp.broadcast_to(totals, (columns, LANES)), 0.0)
        return jnp.broadcast_to(jnp.sum(picked, axis=1, keepdims=True) * (1.0 / total_points), (columns, LANES))

    inner_mean, square_mean, energy_mean = column(0), column(1), column(2)
    projection = inner_mean / (square_mean + EPSILON)
    energy = energy_mean - 2.0 * projection * inner_mean + projection * projection * square_mean
    spread = jnp.sqrt(energy + EPSILON)
    inverse = 1.0 / spread
    arn_ref[0] = projection
    arn_ref[1] = spread

    rows_each = rs_send.shape[1]
    factor = math.sqrt(SKETCH / total_points)
    lowest = HIGH * columns
    part_tiles = LOW // LANES
    for n in range(devices):
        flat = n * rows_each
        tile, row = flat // 8, flat % 8
        strip, side = tile // part_tiles, tile % part_tiles
        top = strip * 8 + row
        q0 = top % columns
        cols = slice(side * LANES, (side + 1) * LANES)
        img = ski[top:top + rows_each, cols] + ski[lowest + top:lowest + top + rows_each, cols]
        bas = skb[top:top + rows_each, cols] + skb[lowest + top:lowest + top + rows_each, cols]
        rs_send[n] = (img - projection[q0:q0 + rows_each] * bas) * (factor * inverse[q0:q0 + rows_each])
    to_all(lambda d: rs_send.at[d], rs_recv, r_ss, r_rs, start)
    rs_recv[me] = rs_send[me]

    for s in range(LEAF):
        pts_rows = (part[s * columns:(s + 1) * columns, :] - projection * nbt[s]) * inverse
        nbt[s] = pts_rows
    for q in range(columns):
        for s in range(LEAF):
            pts[q, s:s + 1, :] = nbt[s, q:q + 1, :]
    for i in range(columns // 4):
        for j in range(4):
            for g in range(4):
                tbuf[0, 32 * g:32 * g + 32, 32 * j:32 * j + 32] = pts[4 * i + j, :, 32 * g:32 * g + 32]
        nb_ref[4 * i:4 * i + 4] = tbuf[0].T.reshape(4, 32, LANES)

    to_all(lambda d: rs_send.at[d], rs_recv, r_ss, r_rs, finish_recv)
    own_chunk[...] = jnp.sum(rs_recv[...], axis=0)
    to_all(lambda d: own_chunk, ag_recv, g_ss, g_rs, start)
    ag_recv[me] = own_chunk[...]
    to_all(lambda d: sum_send, sum_recv, s_ss, s_rs, finish_send)
    to_all(lambda d: rs_send.at[d], rs_recv, r_ss, r_rs, finish_send)
    to_all(lambda d: own_chunk, ag_recv, g_ss, g_rs, finish_recv)
    for n in range(devices):
        flat = n * rows_each
        tile, row = flat // 8, flat % 8
        strip, side = tile // part_tiles, tile % part_tiles
        top = strip * 8 + row
        q0, high = top % columns, top // columns
        begin = high * LOW + side * LANES
        sketch_ref[q0:q0 + rows_each, begin:begin + LANES] = ag_recv[n]
    to_all(lambda d: own_chunk, ag_recv, g_ss, g_rs, finish_send)


def body(basis_vector, diagonal, coords, phase_scale, sketch_rows, sketch_signs):
    columns, local_points = basis_vector.shape
    devices = lax.axis_size("box")
    sections = devices.bit_length() - 1
    count = -(-sections // 5)
    stages, low = [], 0
    for i in range(count):
        bits = (sections - low) // (count - i)
        stages.append((low, bits))
        low += bits
    group = 2 ** max(bits for _, bits in stages)
    group_rows = [columns * WIDTH // LANES * (LANES // 2 ** bits) for _, bits in stages]
    extra = jnp.concatenate([
        coords.astype(F32), diagonal[None, :], sketch_rows.astype(F32)[None, :],
        sketch_signs.astype(F32)[None, :], jnp.zeros((3, local_points), F32)], axis=0)
    stacked = jnp.concatenate([basis_vector, extra], axis=0).reshape(columns + 8, local_points // LANES, LANES)
    rows_each = HIGH * columns * LOW // LANES // devices
    vmem = pl.BlockSpec(memory_space=pltpu.VMEM)
    dma = pltpu.SemaphoreType.DMA
    count_rows = max(group_rows)
    new_basis, sketch, arn = pl.pallas_call(
        functools.partial(kernel, devices, stages, local_points * devices),
        out_shape=(
            jax.ShapeDtypeStruct((columns, local_points // LANES, LANES), F32),
            jax.ShapeDtypeStruct((columns, SKETCH), F32),
            jax.ShapeDtypeStruct((2, columns, LANES), F32)),
        in_specs=[pl.BlockSpec(memory_space=pltpu.SMEM), vmem],
        out_specs=(vmem, vmem, vmem),
        scratch_shapes=[
            pltpu.VMEM((columns + 8, LEAF, LANES), F32),
            pltpu.VMEM((LEAF, WIDTH, LANES), F32),
            pltpu.VMEM((2 * sections, WIDTH, WIDTH, LANES), F32),
            pltpu.VMEM((LEAF, columns, LANES), F32),
            pltpu.VMEM((columns * WIDTH, LANES), F32),
            pltpu.VMEM((columns * WIDTH, LANES), F32),
            pltpu.VMEM((columns * WIDTH // LANES, LANES, LANES), F32),
            pltpu.VMEM((2, LEAF, LANES), F32),
            pltpu.VMEM((LEAF // 4, LOW, 4 * LANES), BF16),
            pltpu.VMEM((2 * HIGH * columns, LOW), F32),
            pltpu.VMEM((2 * HIGH * columns, LOW), F32),
            pltpu.VMEM((count, group, count_rows, LANES), F32),
            pltpu.VMEM((count, group, count_rows, LANES), F32),
            pltpu.VMEM((count, group, count_rows, LANES), F32),
            pltpu.VMEM((count, group, count_rows, LANES), F32),
            pltpu.VMEM((1, LANES), F32),
            pltpu.VMEM((devices, 1, LANES), F32),
            pltpu.VMEM((devices, rows_each, LANES), F32),
            pltpu.VMEM((devices, rows_each, LANES), F32),
            pltpu.VMEM((devices, rows_each, LANES), F32),
            pltpu.VMEM((rows_each, LANES), F32),
            dma((count, group)), dma((count, group)), dma((count, group)), dma((count, group)),
            dma((devices,)), dma((devices,)), dma((devices,)), dma((devices,)), dma((devices,)), dma((devices,)),
        ],
        compiler_params=pltpu.CompilerParams(
            collective_id=0, has_side_effects=True, vmem_limit_bytes=60 * 2**20),
        name="gmres",
    )(phase_scale, stacked)
    return new_basis.reshape(columns, local_points), sketch, arn[:, :, 0]


def solution(mesh):
    placed = (P(None, "box"), P("box"), P(None, "box"), P(), P("box"), P("box"))
    return jax.shard_map(
        body, mesh=mesh, in_specs=placed, out_specs=(P(None, "box"), P(), P()), check_vma=False
    )
```

time: 361 us -> 63.1 us (0.17); the launches traced: 354 us -> 62.6 us
  matrix products: 172 us -> 0 us
  waiting for transfers between devices: 83.7 us -> 0 us
  Pallas kernels: 0 us -> 54.1 us
  blocking collectives: 38.2 us -> 0 us
  local copies, waits for them, and re-layouts: 24.3 us -> 7.13 us
  between operations: 15.3 us -> 1.36 us
  other arithmetic: 11.3 us -> 0.02 us
  starting transfers between devices: 8.69 us -> 0 us
    dot_general x28 -> x0, matrix products: 172 us -> none  [the longest x10 141 us: mix(): jnp.einsum('wvg,vgq->wgq', matrix, coeffs, precision=lax.Precision.HIGHEST)]
    psum x1 -> x0, waiting for transfers between devices: 83.7 us -> none  [body(): lax.psum((sketch_of(image), sketch_of(basis_vector), jnp.sum(basis_vector...]
    pallas_call x0 -> x1, Pallas kernels: none -> 54.1 us  [body(): pl.pallas_call(functools.partial(kernel, devices, stages, local_points *...]
    psum x1 -> x0, blocking collectives: 38.2 us -> none  [body(): lax.psum((sketch_of(image), sketch_of(basis_vector), jnp.sum(basis_vector...]
    ppermute x5 -> x0, local copies, waits for them, and re-layouts: 11.1 us -> none  [swapped(): lax.ppermute(x, axis, [(i, i ^ 1 << bit) for i in range(lax.axis_size(axi...]
    ppermute x5 -> x0, starting transfers between devices: 8.65 us -> none  [swapped(): lax.ppermute(x, axis, [(i, i ^ 1 << bit) for i in range(lax.axis_size(axi...]
    unnamed x16 -> x20, local copies, waits for them, and re-layouts: 1.31 us -> 6.48 us
    add x4 -> x0, local copies, waits for them, and re-layouts: 4.69 us -> none  [one_segment(): return mix(own_map, coeffs) + mix(cross_map, partner)]
  transfers between devices with their start and end apart: 6 -> 0, of which waited for: 1 -> 0; matrix products, arithmetic and copies ran while one was open for 23% -> 0% of each run, Pallas kernels for 0% -> 0%
where the time goes in v1:
time: 63.1 us; the launch traced here: 62.6 us
  Pallas kernels  54.1 us (86%)
  local copies, waits for them, and re-layouts  7.13 us (11%)
  between operations  1.36 us (2%)
    pallas_call x1, Pallas kernels, body(): pl.pallas_call(functools.partial(kernel, devices, stages, local_points *...  54.1 us
    unnamed x20, local copies, waits for them, and re-layouts  6.48 us

profile of v1, /device:TPU:0, one launch (start us, length us, event | category | flops | bytes accessed | tf_op | source)
XLA Modules:
  0.0 62.6 jit_solution(1799895141688805673)
XLA Ops:
  0.6 1.0 %copy.9 = f32[2,8,32,128]{3,2,1,0:T(8,128)S(1)} copy(f32[2,8,32,128]{3,1,2,0:T(8,128)} %bitcast.17) | data formatting | bytes 524288
  1.6 0.0 copy-start.2
  1.7 0.7 %copy-done.2 = s32[2,4096]{1,0:T(2,128)S(1)} copy-done((s32[2,4096]{1,0:T(2,128)S(1)}, s32[2,4096]{1,0:T(2,128)}, u32[]{:S(2)}) %copy-start.2) | copy-done | bytes 32792
  2.4 0.0 copy-start.3
  2.4 0.7 %copy-done.3 = f32[4096]{0:T(1024)S(1)} copy-done((f32[4096]{0:T(1024)S(1)}, f32[4096]{0:T(1024)}, u32[]{:S(2)}) %copy-start.3) | copy-done | bytes 16408
  3.1 0.0 copy-start.4
  3.1 0.7 %copy-done.4 = s32[4096]{0:T(1024)S(1)} copy-done((s32[4096]{0:T(1024)S(1)}, s32[4096]{0:T(1024)}, u32[]{:S(2)}) %copy-start.4) | copy-done | bytes 16408
  3.9 0.0 copy-start.5
  3.9 0.7 %copy-done.5 = s32[4096]{0:T(1024)S(1)} copy-done((s32[4096]{0:T(1024)S(1)}, s32[4096]{0:T(1024)}, u32[]{:S(2)}) %copy-start.5) | copy-done | bytes 16408
  4.6 0.0 copy-start
  5.2 0.1 copy-done
  5.3 54.1 %gmres.1 = (f32[16,32,128]{2,1,0:T(8,128)}, f32[16,2048]{1,0:T(8,128)}, f32[2,16,128]{2,1,0:T(8,128)}) custom-call(s32[1]{0:T(128)S(6)} %copy.21.scale_ref, f32[24,32,128]{2,1,0:T(8,128)} %copy-done), custom_call_target="tpu_custom_call" | custom-call | tf_op jit(solution)/shard_map/gmres/pallas_call | solution.py:393
  59.5 0.0 copy-start.6
  59.5 0.0 copy-start.1
  59.5 1.8 %copy.14 = f32[2,8,32,128]{3,1,2,0:T(8,128)} copy(f32[2,8,32,128]{3,2,1,0:T(8,128)} %bitcast.19) | data formatting | bytes 524288
  61.3 0.0 copy-done.6
  61.3 0.6 %slice_reduce_fusion = f32[2,16]{1,0:T(2,128)} fusion(f32[2,16,128]{2,1,0:T(8,128)S(1)} %copy-done.6), kind=kLoop, calls=%fused_computation.7 | loop fusion | bytes 256 | tf_op jit(solution)/shard_map/slice | solution.py:430
  62.0 0.0 copy-done.1
  62.0 0.7 %copy.22 = f32[16,2048]{1,0:T(8,128)} copy(f32[16,2048]{1,0:T(8,128)S(1)} %copy-done.1) | data formatting | bytes 262144
  (7 shorter events, 0.0 us)
Async XLA Ops:
  1.6 0.8 %copy-start.2 = (s32[2,4096]{1,0:T(2,128)S(1)}, s32[2,4096]{1,0:T(2,128)}, u32[]{:S(2)}) copy-start(s32[2,4096]{1,0:T(2,128)} %param.8) | copy-start | bytes 98308
  2.4 0.7 %copy-start.3 = (f32[4096]{0:T(1024)S(1)}, f32[4096]{0:T(1024)}, u32[]{:S(2)}) copy-start(f32[4096]{0:T(1024)} %param.7) | copy-start | bytes 49156
  3.1 0.7 %copy-start.4 = (s32[4096]{0:T(1024)S(1)}, s32[4096]{0:T(1024)}, u32[]{:S(2)}) copy-start(s32[4096]{0:T(1024)} %param.10) | copy-start | bytes 49156
  3.9 0.7 %copy-start.5 = (s32[4096]{0:T(1024)S(1)}, s32[4096]{0:T(1024)}, u32[]{:S(2)}) copy-start(s32[4096]{0:T(1024)} %param.11) | copy-start | bytes 49156
  4.6 0.7 %copy-start = (f32[24,32,128]{2,1,0:T(8,128)}, f32[24,32,128]{2,1,0:T(8,128)S(1)}, u32[]{:S(2)}) copy-start(f32[24,32,128]{2,1,0:T(8,128)S(1)} %broadcast_dynamic-update-slice_fusion.x_ref) | copy-start | bytes 1179652
  59.5 1.9 %copy-start.6 = (f32[2,16,128]{2,1,0:T(8,128)S(1)}, f32[2,16,128]{2,1,0:T(8,128)}, u32[]{:S(2)}) copy-start(f32[2,16,128]{2,1,0:T(8,128)} %get-tuple-element.8) | copy-start | bytes 49156
  59.5 2.5 %copy-start.1 = (f32[16,2048]{1,0:T(8,128)S(1)}, f32[16,2048]{1,0:T(8,128)}, u32[]{:S(2)}) copy-start(f32[16,2048]{1,0:T(8,128)} %get-tuple-element.13) | copy-start | bytes 393220

commit v2 on v1

--- a/solution.py
+++ b/solution.py
@@ -58,8 +58,8 @@
     return (p & MODULUS) + lax.shift_right_logical(p, 13)
 
 
-def kernel(devices, stages, total_points, scale_ref, x_ref, nb_ref, sketch_ref, arn_ref,
-           pts, leaf, mats, kk, cbuf, part, tbuf, work, onehot, skb, ski,
+def kernel(devices, stages, total_points, scale_ref, v_ref, coords_ref, diag_ref, rows_ref, signs_ref,
+           nb_ref, sketch_ref, arn_ref, raw, pts, leaf, mats, kk, cbuf, part, tbuf, work, onehot, skb, ski,
            a_send, a_recv, b_send, b_recv, sum_send, sum_recv, rs_send, rs_recv, ag_recv, own_chunk,
            a_ss, a_rs, b_ss, b_rs, s_ss, s_rs, r_ss, r_rs, g_ss, g_rs):
     me = lax.axis_index("box")
@@ -75,9 +75,19 @@
     sub = lax.broadcasted_iota(jnp.int32, (8, LANES), 0)
     scale = lax.rem(scale_ref[0], MODULUS)
 
-    rows_in = x_ref.shape[0]
-    for i in range(rows_in // 4):
-        flipped = x_ref[4 * i:4 * i + 4].reshape(LANES, LANES).T
+    for r in range(LANES // 4):
+        here = slice(LANES * r, LANES * (r + 1))
+        for h in range(halves):
+            raw[pl.ds(256 * h + r, 8, stride=32), :] = v_ref[8 * h:8 * h + 8, here]
+        pair = coords_ref[:, here].astype(F32)
+        raw[columns * 32 + r:columns * 32 + r + 1, :] = pair[0:1]
+        raw[columns * 32 + 32 + r:columns * 32 + 33 + r, :] = pair[1:2]
+    raw[(columns + 2) * 32:(columns + 3) * 32, :] = diag_ref[...]
+    raw[(columns + 3) * 32:(columns + 4) * 32, :] = rows_ref[...].astype(F32)
+    raw[(columns + 4) * 32:(columns + 5) * 32, :] = signs_ref[...].astype(F32)
+    raw[(columns + 5) * 32:(columns + 8) * 32, :] = jnp.zeros((96, LANES), F32)
+    for i in range((columns + 8) // 4):
+        flipped = raw[LANES * i:LANES * (i + 1), :].T
         tbuf[0] = flipped
         for j in range(4):
             pts[4 * i + j] = jnp.concatenate(
@@ -101,7 +111,7 @@
             leaf[s, 8 * tile:8 * tile + 8] = scaled_cos(n, unit)
             leaf[s, 16 + 8 * tile:24 + 8 * tile] = scaled_sin(n, unit)
 
-    for h in range(halves):
+    def gather_half(h):
         def gather(s, acc):
             tiles = [leaf[s, 8 * t:8 * t + 8] for t in range(4)]
             out = []
@@ -116,7 +126,7 @@
             for t in range(4):
                 cbuf[pl.ds((8 * h + q) * 32 + 8 * t, 8), :] = acc[4 * q + t]
 
-    blocks = columns * WIDTH // LANES
+    blocks = 8 * WIDTH // LANES
 
     def make_maps(low, bits):
         group = 2 ** bits
@@ -167,21 +177,23 @@
             action(copy)
         return mine
 
-    def pack(send, group):
+    def pack(send, group, h):
         places = LANES // group
         for j in range(blocks):
-            tbuf[j] = cbuf[LANES * j:LANES * (j + 1), :].T
+            at = LANES * (blocks * h + j)
+            tbuf[j] = cbuf[at:at + LANES, :].T
         for d in range(group):
             for j in range(blocks):
                 send[d, places * j:places * (j + 1), :] = tbuf[j, places * d:places * (d + 1), :]
 
-    def unpack(recv, group):
+    def unpack(recv, group, h):
         places = LANES // group
         for j in range(blocks):
             for d in range(group):
                 tbuf[j, places * d:places * (d + 1), :] = recv[d, places * j:places * (j + 1), :]
         for j in range(blocks):
-            cbuf[LANES * j:LANES * (j + 1), :] = tbuf[j].T
+            at = LANES * (blocks * h + j)
+            cbuf[at:at + LANES, :] = tbuf[j].T
 
     def sketch_of(values, target, make):
         target[...] = jnp.zeros_like(target)
@@ -218,29 +230,45 @@
     def finish_send(copy):
         copy.wait_send()
 
-    pl.semaphore_wait(barrier, devices - 1)
     for index, (low, bits) in enumerate(stages):
         group = 2 ** bits
         places = LANES // group
-        send, recv, ssem, rsem = a_send.at[index], a_recv.at[index], a_ss.at[index], a_rs.at[index]
-        pack(send, group)
-        mine = exchange(send, recv, ssem, rsem, low, bits, start)
-        recv[mine] = send[mine]
+
+        def outward(h, action):
+            at = halves * index + h
+            return exchange(a_send.at[at], a_recv.at[at], a_ss.at[at], a_rs.at[at], low, bits, action)
+
+        def homeward(h, action):
+            at = halves * index + h
+            return exchange(b_send.at[at], b_recv.at[at], b_ss.at[at], b_rs.at[at], low, bits, action)
+
+        for h in range(halves):
+            at = halves * index + h
+            if index == 0:
+                gather_half(h)
+            pack(a_send.at[at], group, h)
+            if index == 0 and h == 0:
+                pl.semaphore_wait(barrier, devices - 1)
+            mine = outward(h, start)
+            a_recv[at, mine] = a_send[at, mine]
         make_maps(low, bits)
         if index == 0:
             for q in range(columns):
                 for s in range(LEAF):
                     nbt[s, q:q + 1, :] = pts[q, s:s + 1, :]
             sketch_of(lambda s: nbt[s], skb, True)
-        exchange(send, recv, ssem, rsem, low, bits, finish_recv)
-        unpack(recv, group)
-        for k in range(low, low + bits):
-            span = places * 2 ** (k - low)
-            full = cbuf[...]
-            wide = lax.broadcasted_iota(jnp.int32, full.shape, 1)
-            part[...] = jnp.where((wide // span) % 2 == 0,
-                                  pltpu.roll(full, LANES - span, 1), pltpu.roll(full, span, 1))
-            for h in range(halves):
+        for h in range(halves):
+            at = halves * index + h
+            outward(h, finish_recv)
+            unpack(a_recv.at[at], group, h)
+            half = slice(256 * h, 256 * (h + 1))
+            for k in range(low, low + bits):
+                span = places * 2 ** (k - low)
+                full = cbuf[half, :]
+                wide = lax.broadcasted_iota(jnp.int32, full.shape, 1)
+                part[half, :] = jnp.where((wide // span) % 2 == 0,
+                                          pltpu.roll(full, LANES - span, 1), pltpu.roll(full, span, 1))
+
                 def mix(v, acc):
                     own = [mats[2 * k, v, 8 * t:8 * t + 8] for t in range(4)]
                     cross = [mats[2 * k + 1, v, 8 * t:8 * t + 8] for t in range(4)]
@@ -257,14 +285,16 @@
                 for q in range(8):
                     for t in range(4):
                         cbuf[pl.ds((8 * h + q) * 32 + 8 * t, 8), :] = acc[4 * q + t]
-        exchange(send, recv, ssem, rsem, low, bits, finish_send)
-        send, recv, ssem, rsem = b_send.at[index], b_recv.at[index], b_ss.at[index], b_rs.at[index]
-        pack(send, group)
-        mine = exchange(send, recv, ssem, rsem, low, bits, start)
-        recv[mine] = send[mine]
-        exchange(send, recv, ssem, rsem, low, bits, finish_recv)
-        unpack(recv, group)
-        exchange(send, recv, ssem, rsem, low, bits, finish_send)
+            pack(b_send.at[at], group, h)
+            mine = homeward(h, start)
+            b_recv[at, mine] = b_send[at, mine]
+        for h in range(halves):
+            outward(h, finish_send)
+        for h in range(halves):
+            homeward(h, finish_recv)
+            unpack(b_recv.at[halves * index + h], group, h)
+        for h in range(halves):
+            homeward(h, finish_send)
 
     for c in range(LEAF // 8):
         def spread_out(w, acc):
@@ -320,8 +350,8 @@
     energy = energy_mean - 2.0 * projection * inner_mean + projection * projection * square_mean
     spread = jnp.sqrt(energy + EPSILON)
     inverse = 1.0 / spread
-    arn_ref[0] = projection
-    arn_ref[1] = spread
+    for i, value in enumerate((projection, spread)):
+        arn_ref[i:i + 1, :] = jnp.sum(jnp.where(lane_q == row_q, value, 0.0), axis=0, keepdims=True)[:, :columns]
 
     rows_each = rs_send.shape[1]
     factor = math.sqrt(SKETCH / total_points)
@@ -350,7 +380,10 @@
         for j in range(4):
             for g in range(4):
                 tbuf[0, 32 * g:32 * g + 32, 32 * j:32 * j + 32] = pts[4 * i + j, :, 32 * g:32 * g + 32]
-        nb_ref[4 * i:4 * i + 4] = tbuf[0].T.reshape(4, 32, LANES)
+        raw[LANES * i:LANES * (i + 1), :] = tbuf[0].T
+    for r in range(LANES // 4):
+        for h in range(halves):
+            nb_ref[8 * h:8 * h + 8, LANES * r:LANES * (r + 1)] = raw[pl.ds(256 * h + r, 8, stride=32), :]
 
     to_all(lambda d: rs_send.at[d], rs_recv, r_ss, r_rs, finish_recv)
     own_chunk[...] = jnp.sum(rs_recv[...], axis=0)
@@ -382,23 +415,22 @@
         low += bits
     group = 2 ** max(bits for _, bits in stages)
     group_rows = [columns * WIDTH // LANES * (LANES // 2 ** bits) for _, bits in stages]
-    extra = jnp.concatenate([
-        coords.astype(F32), diagonal[None, :], sketch_rows.astype(F32)[None, :],
-        sketch_signs.astype(F32)[None, :], jnp.zeros((3, local_points), F32)], axis=0)
-    stacked = jnp.concatenate([basis_vector, extra], axis=0).reshape(columns + 8, local_points // LANES, LANES)
+    plane = (local_points // LANES, LANES)
     rows_each = HIGH * columns * LOW // LANES // devices
     vmem = pl.BlockSpec(memory_space=pltpu.VMEM)
     dma = pltpu.SemaphoreType.DMA
     count_rows = max(group_rows)
+    halves = columns // 8
     new_basis, sketch, arn = pl.pallas_call(
         functools.partial(kernel, devices, stages, local_points * devices),
         out_shape=(
-            jax.ShapeDtypeStruct((columns, local_points // LANES, LANES), F32),
+            jax.ShapeDtypeStruct((columns, local_points), F32),
             jax.ShapeDtypeStruct((columns, SKETCH), F32),
-            jax.ShapeDtypeStruct((2, columns, LANES), F32)),
-        in_specs=[pl.BlockSpec(memory_space=pltpu.SMEM), vmem],
+            jax.ShapeDtypeStruct((2, columns), F32)),
+        in_specs=[pl.BlockSpec(memory_space=pltpu.SMEM), vmem, vmem, vmem, vmem, vmem],
         out_specs=(vmem, vmem, vmem),
         scratch_shapes=[
+            pltpu.VMEM(((columns + 8) * LEAF, LANES), F32),
             pltpu.VMEM((columns + 8, LEAF, LANES), F32),
             pltpu.VMEM((LEAF, WIDTH, LANES), F32),
             pltpu.VMEM((2 * sections, WIDTH, WIDTH, LANES), F32),
@@ -410,24 +442,25 @@
             pltpu.VMEM((LEAF // 4, LOW, 4 * LANES), BF16),
             pltpu.VMEM((2 * HIGH * columns, LOW), F32),
             pltpu.VMEM((2 * HIGH * columns, LOW), F32),
-            pltpu.VMEM((count, group, count_rows, LANES), F32),
-            pltpu.VMEM((count, group, count_rows, LANES), F32),
-            pltpu.VMEM((count, group, count_rows, LANES), F32),
-            pltpu.VMEM((count, group, count_rows, LANES), F32),
+            pltpu.VMEM((count * halves, group, count_rows // halves, LANES), F32),
+            pltpu.VMEM((count * halves, group, count_rows // halves, LANES), F32),
+            pltpu.VMEM((count * halves, group, count_rows // halves, LANES), F32),
+            pltpu.VMEM((count * halves, group, count_rows // halves, LANES), F32),
             pltpu.VMEM((1, LANES), F32),
             pltpu.VMEM((devices, 1, LANES), F32),
             pltpu.VMEM((devices, rows_each, LANES), F32),
             pltpu.VMEM((devices, rows_each, LANES), F32),
             pltpu.VMEM((devices, rows_each, LANES), F32),
             pltpu.VMEM((rows_each, LANES), F32),
-            dma((count, group)), dma((count, group)), dma((count, group)), dma((count, group)),
+            dma((count * halves, group)), dma((count * halves, group)), dma((count * halves, group)), dma((count * halves, group)),
             dma((devices,)), dma((devices,)), dma((devices,)), dma((devices,)), dma((devices,)), dma((devices,)),
         ],
         compiler_params=pltpu.CompilerParams(
             collective_id=0, has_side_effects=True, vmem_limit_bytes=60 * 2**20),
         name="gmres",
-    )(phase_scale, stacked)
-    return new_basis.reshape(columns, local_points), sketch, arn[:, :, 0]
+    )(phase_scale, basis_vector, coords, diagonal.reshape(plane), sketch_rows.reshape(plane),
+      sketch_signs.reshape(plane))
+    return new_basis, sketch, arn
 
 
 def solution(mesh):

time: 63.1 us -> 58.7 us (0.930)
  local copies, waits for them, and re-layouts: 7.13 us -> 2.93 us
    unnamed x20 -> x7, local copies, waits for them, and re-layouts: 6.48 us -> 2.93 us
    slice x1 -> x0, local copies, waits for them, and re-layouts: 0.65 us -> none  [body(): return (new_basis.reshape(columns, local_points), sketch, arn[:, :, 0])]
where the time goes in v2:
time: 58.7 us; the launch traced here: 58.6 us
  Pallas kernels  54.3 us (93%)
  local copies, waits for them, and re-layouts  2.93 us (5%)
  between operations  1.3 us (2%)
    pallas_call x1, Pallas kernels, body(): pl.pallas_call(functools.partial(kernel, devices, stages, local_points *...  54.3 us
    unnamed x7, local copies, waits for them, and re-layouts  2.93 us

profile of v2, /device:TPU:0, one launch (start us, length us, event | category | flops | bytes accessed | tf_op | source)
XLA Modules:
  0.0 58.6 jit_solution(8470592065461624052)
XLA Ops:
  1.3 54.3 %gmres.1 = (f32[16,4096]{1,0:T(8,128)}, f32[16,2048]{1,0:T(8,128)}, f32[2,16]{1,0:T(2,128)}) custom-call(s32[1]{0:T(128)S(6)} %copy.12.scale_ref, f32[16,4096]{1,0:T(8,128)} %v_ref.1, s32[2,4096]{1,0:T(2,128)} %coords_ref.1, f32[32,128]{1,0:T(8,128)} %bitcast.3, s32[32,128]{1,0:T(8,128)} %bitcast.4, s32[32,128]{1,0:T(8,128)} %bitcast.5), custom_call_target="tpu_custom_call" | custom-call | tf_op jit(solution)/shard_map/gmres/pallas_call | solution.py:424
  55.6 0.0 copy-start
  55.6 1.7 %copy.13 = f32[16,4096]{1,0:T(8,128)} copy(f32[16,4096]{1,0:T(8,128)} %get-tuple-element.6) | data formatting | bytes 524288
  57.3 0.0 copy-done
  57.3 0.0 copy-start.1
  57.3 0.7 %copy.14 = f32[16,2048]{1,0:T(8,128)} copy(f32[16,2048]{1,0:T(8,128)S(1)} %copy-done) | data formatting | bytes 262144
  58.0 0.0 copy-done.1
  58.0 0.6 copy.15
Async XLA Ops:
  55.6 1.7 %copy-start = (f32[16,2048]{1,0:T(8,128)S(1)}, f32[16,2048]{1,0:T(8,128)}, u32[]{:S(2)}) copy-start(f32[16,2048]{1,0:T(8,128)} %get-tuple-element.7) | copy-start | bytes 393220
  57.3 0.7 %copy-start.1 = (f32[2,16]{1,0:T(2,128)S(1)}, f32[2,16]{1,0:T(2,128)}, u32[]{:S(2)}) copy-start(f32[2,16]{1,0:T(2,128)} %get-tuple-element.8) | copy-start | bytes 388
